TPU v7x, 32 devices: a whole 2x2x4 slice. The times are simulated.
32 devices in a mesh: dp: 8 (over y, x, core), expert: 4 (over z).
Axes of the slice: x: 2, y: 2, z: 4, core: 2. Of those that a mesh axis runs over, the one named last changes fastest.
Arguments:
- cotangent: bfloat16 [32768, 2048], P(('dp', 'expert')), may hold values from -6 to 6
- route_ids: int32 [32768, 6], P(('dp', 'expert')), may hold values from 0 to 63, all different within a row; in each aligned block of 1024 rows (0 to 1023, 1024 to 2047, ...) at most 192 rows name the same one
- route_weights: float32 [32768, 6], P(('dp', 'expert')), may hold values from 0.02 to 1
- hidden: bfloat16 [8, 6144, 1408], P('expert', 'dp'), may hold values from -6 to 6
- master: float32 [1408, 8, 2048], P('dp', 'expert'), may hold values from -0.3 to 0.3
- first_moment: float32 [1408, 8, 2048], P('dp', 'expert'), may hold values from -1.2 to 1.2
- second_moment: float32 [1408, 8, 2048], P('dp', 'expert'), may hold values from 0.002 to 0.05
Outputs:
- new_master: float32 [1408, 8, 2048], P('dp', 'expert')
- new_first: float32 [1408, 8, 2048], P('dp', 'expert')
- new_second: float32 [1408, 8, 2048], P('dp', 'expert')
Inputs may be any that keep to these rules, and one draw needn't show every extreme that they name: `route_ids`: each row names 6 different experts. Within the 1024 rows of one device no expert is named by more than 192 rows.
All inputs are finite; a program needn't handle non-finite values.
Results may differ from a plain program's by a relative error of at most 0.0019.
Values may be sent and summed in bfloat16 or wider, within the bound.
A program may use at most 128 MiB of HBM per device.

v0:
```python
import jax
import jax.numpy as jnp
from jax import lax
from jax.sharding import PartitionSpec as P

beta_one = 0.9
beta_two = 0.999
learning_rate = 0.001
epsilon = 1e-08
decay_rate = 0.1
step_count = 4.0


def slot_table(route_ids, route_weights, window, capacity, local_count, groups):
    tokens = route_ids.shape[0]
    onehot = (route_ids[:, :, None] == jnp.arange(window, dtype=jnp.int32)[None, None, :]).astype(
        jnp.int32
    )
    counts = jnp.sum(onehot, axis=1)
    before = jnp.cumsum(counts, axis=0) - counts
    ranks = jnp.sum(onehot * before[:, None, :], axis=2)
    inside = route_ids < window
    position = (
        route_ids % local_count * (groups * capacity) + route_ids // local_count * capacity + ranks
    )
    position = jnp.where(inside, position, window * capacity)
    anchor = jnp.broadcast_to(jnp.arange(tokens, dtype=jnp.int32)[:, None], route_ids.shape)
    slot_anchor = (
        jnp.zeros((window * capacity + 1,), jnp.int32)
        .at[position.reshape(-1)]
        .set(anchor.reshape(-1))
    )
    masked = jnp.where(inside, route_weights, jnp.zeros_like(route_weights))
    slot_weight = (
        jnp.zeros((window * capacity + 1,), route_weights.dtype)
        .at[position.reshape(-1)]
        .set(masked.reshape(-1))
    )
    return (slot_anchor[:-1], slot_weight[:-1])


def shards(cotangent, route_ids, route_weights, hidden, master, first_moment, second_moment):
    groups = lax.axis_size("expert")
    local_count = hidden.shape[0]
    capacity = hidden.shape[1] // groups
    width = cotangent.shape[1]
    window = local_count * groups
    owned_rows = master.shape[0]
    slot_anchor, slot_weight = slot_table(
        route_ids, route_weights, window, capacity, local_count, groups
    )
    scaled = (cotangent[slot_anchor].astype(jnp.float32) * slot_weight[:, None]).astype(
        jnp.bfloat16
    )
    scaled = scaled.reshape(local_count, groups * capacity, width)
    received = lax.all_to_all(scaled, "expert", split_axis=1, concat_axis=1, tiled=True)
    pieces = []
    for expert_local in range(local_count):
        hidden_one = hidden[expert_local]
        received_one = received[expert_local]

        def one_term(start, count, hidden_one=hidden_one, received_one=received_one):
            return jnp.einsum(
                "rf,rd->fd", hidden_one, received_one, preferred_element_type=jnp.float32
            )

        pieces.append(
            lax.psum_scatter(
                one_term(jnp.int32(0), owned_rows * lax.axis_size("dp")),
                "dp",
                scatter_dimension=0,
                tiled=True,
            )
        )
    summed = jnp.stack(pieces, axis=1)
    gradient = summed / jnp.sqrt(jnp.float32(groups * capacity))
    new_first = beta_one * first_moment + (1.0 - beta_one) * gradient
    new_second = beta_two * second_moment + (1.0 - beta_two) * gradient * gradient
    corrected_first = new_first / (1.0 - beta_one**step_count)
    corrected_second = new_second / (1.0 - beta_two**step_count)
    update = corrected_first / (jnp.sqrt(corrected_second) + epsilon) + decay_rate * master
    new_master = master - learning_rate * update
    return (new_master, new_first, new_second)


def solution(mesh):
    placed = (
        P(("dp", "expert"), None),
        P(("dp", "expert"), None),
        P(("dp", "expert"), None),
        P("expert", "dp", None),
        P("dp", "expert", None),
        P("dp", "expert", None),
        P("dp", "expert", None),
    )
    return jax.shard_map(
        shards,
        mesh=mesh,
        in_specs=placed,
        out_specs=(P("dp", "expert", None), P("dp", "expert", None), P("dp", "expert", None)),
        check_vma=False,
    )
```

profile of v0, /device:TPU:0, one launch (start us, length us, event | category | flops | bytes accessed | tf_op | source)
XLA Modules:
  0.0 474.1 jit_solution(2417612220993016401)
XLA Ops:
  7.2 0.8 convert_reduce_fusion
  8.0 2.3 reduce-window.6
  10.8 0.8 select_reduce_fusion
  11.7 0.8 fusion.10
  12.5 0.8 broadcast_select_fusion
  13.5 0.3 reshape.92
  14.0 0.4 reshape.68
  14.5 23.0 %scatter_custom_fusion.1 = f32[1537]{0:T(1024)S(1)} fusion(s32[6144]{0:T(1024)S(1)} %bitcast.45, f32[6144]{0:T(1024)S(1)} %reshape.92, f32[]{:T(128)} %constant.62.clone.1), kind=kCustom, calls=%fused_computation.46 | custom fusion | bytes 6152 | tf_op jit(solution)/shard_map/scatter | solution.py:37
  37.8 23.0 %scatter_custom_fusion = s32[1537]{0:T(1024)S(1)} fusion(s32[6144]{0:T(1024)S(1)} %bitcast.46, s32[6144]{0:T(1024)S(1)} %reshape.84, s32[]{:T(128)} %constant.29.clone.1), kind=kCustom, calls=%fused_computation.48 | custom fusion | bytes 6152 | tf_op jit(solution)/shard_map/scatter | solution.py:31
  60.9 15.5 %gather_fusion = bf16[1536,2048]{1,0:T(8,128)(2,1)} fusion(bf16[1024,2048]{1,0:T(8,128)(2,1)} %param.7, s32[2048]{0:T(1024)S(1)} %pad_clamp_fusion), kind=kCustom, calls=%fused_computation | custom fusion | bytes 12589056 | tf_op jit(solution)/shard_map/gather | solution.py:52
  76.3 3.9 fusion
  80.2 13.0 %copy.75 = bf16[2,768,2048]{2,0,1:T(2,128)(2,1)S(1)} copy(bf16[2,768,2048]{2,1,0:T(8,128)(2,1)S(1)} %fusion) | data formatting | bytes 12582912 | tf_op jit(solution)/shard_map/convert_element_type | solution.py:52
  93.3 144.5 %all_to_all.5 = bf16[2,768,2048]{2,0,1:T(2,128)(2,1)S(1)} all-to-all(bf16[2,768,2048]{2,0,1:T(2,128)(2,1)S(1)} %copy.75), channel_id=1, replica_groups=mesh['dp'=8,'expert'=4] {'expert'}, dimensions={1} | all-to-all | bytes 12582912 | tf_op jit(solution)/shard_map/all_to_all | solution.py:56
  237.7 9.7 %fusion.23 = (bf16[1,768,2048]{2,0,1:T(2,128)(2,1)S(1)}, bf16[1,768,2048]{2,0,1:T(2,128)(2,1)}) fusion(bf16[2,768,2048]{2,0,1:T(2,128)(2,1)S(1)} %all_to_all.5), kind=kLoop, calls=%fused_computation.50 | loop fusion | bytes 12582912 | tf_op jit(solution)/shard_map/slice | solution.py:60
  247.5 9.6 %convolution_bitcast_fusion.1 = f32[1408,2048]{0,1:T(8,128)} fusion(bf16[1,768,2048]{2,0,1:T(2,128)(2,1)S(1)} %get-tuple-element.24, bf16[2,768,1408]{2,1,0:T(8,128)(2,1)S(1)} %bitcast.49), kind=kOutput, calls=%fused_computation.6 | convolution fusion | flops 4429185024 | bytes 19988480 | tf_op jit(solution)/shard_map/rf,rd->fd/dot_general | solution.py:63
  257.1 12.0 %copy.86 = f32[1408,2048]{1,0:T(8,128)} copy(f32[1408,2048]{0,1:T(8,128)} %convolution_bitcast_fusion.1) | data formatting | bytes 23068672
  269.2 12.6 %convolution_bitcast_fusion = f32[1408,2048]{0,1:T(8,128)} fusion(bf16[1,768,2048]{2,0,1:T(2,128)(2,1)} %get-tuple-element.25, bf16[2,768,1408]{2,1,0:T(8,128)(2,1)} %param.10), kind=kOutput, calls=%fused_computation.5 | convolution fusion | flops 4429185024 | bytes 19988480 | tf_op jit(solution)/shard_map/rf,rd->fd/dot_general | solution.py:63
  281.8 12.8 %copy.88 = f32[1408,2048]{1,0:T(8,128)} copy(f32[1408,2048]{0,1:T(8,128)} %convolution_bitcast_fusion) | data formatting | bytes 23068672
  294.6 61.4 %reduce-scatter.7.cloned.1.call-done = f32[176,2048]{1,0:T(8,128)} async-done(((f32[1408,2048]{1,0:T(8,128)}), f32[176,2048]{1,0:T(8,128)}) %reduce-scatter.7.cloned.1.call-update) | async-done | bytes 1441808 | tf_op jit(solution)/shard_map/reduce_scatter | solution.py:68
  356.0 90.7 %reduce-scatter.9.cloned.1.call-done = f32[176,2048]{1,0:T(8,128)} async-done(((f32[1408,2048]{1,0:T(8,128)}), f32[176,2048]{1,0:T(8,128)}) %reduce-scatter.9.cloned.1.call-update) | async-done | bytes 1441808 | tf_op jit(solution)/shard_map/reduce_scatter | solution.py:68
  446.7 9.2 %multiply_subtract_fusion = (f32[176,2,2048]{2,0,1:T(8,128)S(1)}, f32[176,2,2048]{2,0,1:T(8,128)S(1)}, f32[176,2,2048]{2,0,1:T(8,128)S(1)}) fusion(f32[176,2,2048]{2,1,0:T(2,128)S(1)} %copy-done, f32[176,1,2048]{2,0,1:T(8,128)} %bitcast.42, f32[176,1,2048]{2,0,1:T(8,128)} %bitcast.41, f32[176,2,2048]{2,1,0:T(2,128)} %param.12, f32[176,2,2048]{2,1,0:T(2,128)} %param.13), kind=kLoop, calls=%fused_computation.14 | loop fusion | flops 12255232 | bytes 20185088 | tf_op jit(solution)/shard_map/sub | solution.py:82
  455.9 3.8 copy.83
  459.7 3.8 copy.84
  463.5 3.8 copy.85
  (24 shorter events, 1.5 us)
Async XLA Ops:
  7.2 348.8 %reduce-scatter.7.cloned.1.call-start = ((), (), s32[]{:S(2)}) async-start(), calls=%async_computation.3 | async-start | bytes 12976128 | tf_op jit(solution)/shard_map/reduce_scatter | solution.py:68
  93.2 154.2 %slice-start = ((s8[4325376]{0:T(1024)(128)(4,1)}), s8[4194304]{0:T(1024)(128)(4,1)S(1)}, s32[]{:S(2)}) async-start(s8[4325376]{0:T(1024)(128)(4,1)} %bitcast.48), calls=%async_computation.5 | async-start | bytes 8388608
  237.7 9.7 %slice-start.1 = ((s8[4325376]{0:T(1024)(128)(4,1)}), s8[131072]{0:T(1024)(128)(4,1)S(1)}, s32[]{:S(2)}) async-start(s8[4325376]{0:T(1024)(128)(4,1)} %bitcast.48), calls=%async_computation.6 | async-start | bytes 262144
  269.2 177.5 %reduce-scatter.9.cloned.1.call-start = ((), (), s32[]{:S(2)}) async-start(), calls=%async_computation.4 | async-start | bytes 12976128 | tf_op jit(solution)/shard_map/reduce_scatter | solution.py:68
  294.6 152.1 %copy-start = (f32[176,2,2048]{2,1,0:T(2,128)S(1)}, f32[176,2,2048]{2,1,0:T(2,128)}, u32[]{:S(2)}) copy-start(f32[176,2,2048]{2,1,0:T(2,128)} %param.11) | copy-start | bytes 8650756
Sparse Core Ops, SparseCore 0:
  269.3 86.6 reduce-scatter.6
  359.5 87.1 reduce-scatter.8
where the time goes:
time: 475 us; the launch traced here: 474 us
  waiting for transfers between devices  152 us (32%)
  blocking collectives  144 us (30%)
  local copies, waits for them, and re-layouts  122 us (26%)
  matrix products  22.2 us (5%)
  other arithmetic  18.9 us (4%)
  between operations  14.2 us (3%)
    reduce_scatter x2, waiting for transfers between devices, shards(): lax.psum_scatter(one_term(jnp.int32(0), owned_rows * lax.axis_size('dp'))...  152 us
    all_to_all x1, blocking collectives, shards(): lax.all_to_all(scaled, 'expert', split_axis=1, concat_axis=1, tiled=True)  144 us
    unnamed x11, local copies, waits for them, and re-layouts  36.2 us
    scatter x1, local copies, waits for them, and re-layouts, slot_table(): slot_weight = jnp.zeros((window * capacity + 1,), route_weights.dtype).at...  23 us
    scatter x1, local copies, waits for them, and re-layouts, slot_table(): slot_anchor = jnp.zeros((window * capacity + 1,), jnp.int32).at[position....  23 us
    dot_general x2, matrix products, one_term(): jnp.einsum('rf,rd->fd', hidden_one, received_one, preferred_element_type=...  22.2 us
    gather x1, local copies, waits for them, and re-layouts, shards(): cotangent[slot_anchor].astype(jnp.float32) * slot_weight[:, None]  15.5 us
    convert_element_type x1, local copies, waits for them, and re-layouts, shards(): (cotangent[slot_anchor].astype(jnp.float32) * slot_weight[:, None]).astyp...  13 us
  transfers between devices with their start and end apart: 2, of which 2 were waited for; matrix products, arithmetic and copies ran while one was open for 5% of the time, Pallas kernels for 0%

commit v1 on v0

--- a/solution.py
+++ b/solution.py
@@ -9,6 +9,12 @@
 epsilon = 1e-08
 decay_rate = 0.1
 step_count = 4.0
+
+
+def trade_parts(x, axis, split, join):
+    parts = jnp.split(x, lax.axis_size(axis), axis=split)
+    received = lax.all_to_all(jnp.stack(parts), axis, 0, 0)
+    return jnp.concatenate(received, axis=join)
 
 
 def slot_table(route_ids, route_weights, window, capacity, local_count, groups):
@@ -53,7 +59,7 @@
         jnp.bfloat16
     )
     scaled = scaled.reshape(local_count, groups * capacity, width)
-    received = lax.all_to_all(scaled, "expert", split_axis=1, concat_axis=1, tiled=True)
+    received = trade_parts(scaled, "expert", 1, 1)
     pieces = []
     for expert_local in range(local_count):
         hidden_one = hidden[expert_local]

time: 475 us -> 454 us (0.956)
  local copies, waits for them, and re-layouts: 122 us -> 102 us
    convert_element_type x1 -> x0, local copies, waits for them, and re-layouts: 13 us -> none  [shards(): (cotangent[slot_anchor].astype(jnp.float32) * slot_weight[:, None]).astyp...]
    slice x1, local copies, waits for them, and re-layouts: 9.74 us -> 1.11 us  [shards(): received_one = received[expert_local]]
where the time goes in v1:
time: 454 us; the launch traced here: 453 us
  waiting for transfers between devices  154 us (34%)
  blocking collectives  144 us (32%)
  local copies, waits for them, and re-layouts  102 us (22%)
  other arithmetic  19.7 us (4%)
  matrix products  18.2 us (4%)
  between operations  14.2 us (3%)
    reduce_scatter x2, waiting for transfers between devices, shards(): lax.psum_scatter(one_term(jnp.int32(0), owned_rows * lax.axis_size('dp'))...  154 us
    all_to_all x1, blocking collectives, trade_parts(): received = lax.all_to_all(jnp.stack(parts), axis, 0, 0)  144 us
    unnamed x11, local copies, waits for them, and re-layouts  36.4 us
    scatter x1, local copies, waits for them, and re-layouts, slot_table(): slot_weight = jnp.zeros((window * capacity + 1,), route_weights.dtype).at...  23 us
    scatter x1, local copies, waits for them, and re-layouts, slot_table(): slot_anchor = jnp.zeros((window * capacity + 1,), jnp.int32).at[position....  23 us
    dot_general x2, matrix products, one_term(): jnp.einsum('rf,rd->fd', hidden_one, received_one, preferred_element_type=...  18.2 us
    gather x1, local copies, waits for them, and re-layouts, shards(): cotangent[slot_anchor].astype(jnp.float32) * slot_weight[:, None]  15.5 us
    sub x1, other arithmetic, shards(): new_master = master - learning_rate * update  9.23 us
  transfers between devices with their start and end apart: 2, of which 2 were waited for; matrix products, arithmetic and copies ran while one was open for 5% of the time, Pallas kernels for 0%

profile of v1, /device:TPU:0, one launch (start us, length us, event | category | flops | bytes accessed | tf_op | source)
XLA Modules:
  0.0 452.7 jit_solution(2854656655957121144)
XLA Ops:
  7.2 0.8 convert_reduce_fusion
  8.0 2.3 reduce-window.6
  10.8 0.8 select_reduce_fusion
  11.7 0.8 fusion.10
  12.5 0.8 broadcast_select_fusion
  14.0 0.4 reshape.76
  14.5 23.0 %scatter_custom_fusion.1 = f32[1537]{0:T(1024)S(1)} fusion(s32[6144]{0:T(1024)S(1)} %bitcast.55, f32[6144]{0:T(1024)S(1)} %reshape.101, f32[]{:T(128)} %constant.62.clone.1), kind=kCustom, calls=%fused_computation.49 | custom fusion | bytes 6152 | tf_op jit(solution)/shard_map/scatter | solution.py:43
  37.8 23.0 %scatter_custom_fusion = s32[1537]{0:T(1024)S(1)} fusion(s32[6144]{0:T(1024)S(1)} %bitcast.56, s32[6144]{0:T(1024)S(1)} %reshape.93, s32[]{:T(128)} %constant.29.clone.1), kind=kCustom, calls=%fused_computation.51 | custom fusion | bytes 6152 | tf_op jit(solution)/shard_map/scatter | solution.py:37
  60.9 15.5 %gather_fusion = bf16[1536,2048]{1,0:T(8,128)(2,1)} fusion(bf16[1024,2048]{1,0:T(8,128)(2,1)} %param.7, s32[2048]{0:T(1024)S(1)} %pad_clamp_fusion), kind=kCustom, calls=%fused_computation | custom fusion | bytes 12589056 | tf_op jit(solution)/shard_map/gather | solution.py:58
  76.3 3.9 fusion
  80.2 1.1 slice_bitcast_fusion.3
  81.3 0.8 pad_maximum_fusion
  82.2 144.5 %all_to_all.5 = bf16[4,2,192,2048]{3,2,1,0:T(8,128)(2,1)S(1)} all-to-all(bf16[4,2,192,2048]{3,2,1,0:T(8,128)(2,1)S(1)} %pad_maximum_fusion), channel_id=1, replica_groups=mesh['dp'=8,'expert'=4] {'expert'}, dimensions={0} | all-to-all | bytes 12582912 | tf_op jit(solution)/shard_map/all_to_all | solution.py:16
  226.7 1.1 fusion.23
  227.8 7.8 %convolution_bitcast_fusion = f32[1408,2048]{0,1:T(8,128)} fusion(bf16[768,2048]{1,0:T(8,128)(2,1)S(1)} %bitcast.50, bf16[2,768,1408]{2,1,0:T(8,128)(2,1)S(1)} %bitcast.59), kind=kOutput, calls=%fused_computation.5 | convolution fusion | flops 4429185024 | bytes 16842752 | tf_op jit(solution)/shard_map/rf,rd->fd/dot_general | solution.py:69
  235.7 12.0 %copy.65 = f32[1408,2048]{1,0:T(8,128)} copy(f32[1408,2048]{0,1:T(8,128)} %convolution_bitcast_fusion) | data formatting | bytes 23068672
  247.8 10.4 %convolution_bitcast_fusion.1 = f32[1408,2048]{0,1:T(8,128)} fusion(bf16[768,2048]{1,0:T(8,128)(2,1)S(1)} %bitcast.49, bf16[2,768,1408]{2,1,0:T(8,128)(2,1)} %param.10), kind=kOutput, calls=%fused_computation.6 | convolution fusion | flops 4429185024 | bytes 16842752 | tf_op jit(solution)/shard_map/rf,rd->fd/dot_general | solution.py:69
  258.1 13.0 %copy.63 = f32[1408,2048]{1,0:T(8,128)} copy(f32[1408,2048]{0,1:T(8,128)} %convolution_bitcast_fusion.1) | data formatting | bytes 23068672
  271.1 63.4 %reduce-scatter.9.cloned.1.call-done = f32[176,2048]{1,0:T(8,128)} async-done(((f32[1408,2048]{1,0:T(8,128)}), f32[176,2048]{1,0:T(8,128)}) %reduce-scatter.9.cloned.1.call-update) | async-done | bytes 1441808 | tf_op jit(solution)/shard_map/reduce_scatter | solution.py:74
  334.5 90.7 %reduce-scatter.7.cloned.1.call-done = f32[176,2048]{1,0:T(8,128)} async-done(((f32[1408,2048]{1,0:T(8,128)}), f32[176,2048]{1,0:T(8,128)}) %reduce-scatter.7.cloned.1.call-update) | async-done | bytes 1441808 | tf_op jit(solution)/shard_map/reduce_scatter | solution.py:74
  425.2 9.2 %multiply_subtract_fusion = (f32[176,2,2048]{2,0,1:T(8,128)S(1)}, f32[176,2,2048]{2,0,1:T(8,128)S(1)}, f32[176,2,2048]{2,0,1:T(8,128)S(1)}) fusion(f32[176,2,2048]{2,1,0:T(2,128)S(1)} %copy-done, f32[176,1,2048]{2,0,1:T(8,128)} %bitcast.51, f32[176,1,2048]{2,0,1:T(8,128)} %bitcast.52, f32[176,2,2048]{2,1,0:T(2,128)} %param.12, f32[176,2,2048]{2,1,0:T(2,128)} %param.13), kind=kLoop, calls=%fused_computation.13 | loop fusion | flops 12255232 | bytes 20185088 | tf_op jit(solution)/shard_map/sub | solution.py:88
  434.4 3.8 copy.60
  438.2 3.8 copy.61
  442.1 3.8 copy.62
  (25 shorter events, 1.9 us)
Async XLA Ops:
  7.2 327.4 %reduce-scatter.9.cloned.1.call-start = ((), (), s32[]{:S(2)}) async-start(), calls=%async_computation.4 | async-start | bytes 12976128 | tf_op jit(solution)/shard_map/reduce_scatter | solution.py:74
  82.2 145.6 %slice-start = ((s8[4325376]{0:T(1024)(128)(4,1)}), s8[4194304]{0:T(1024)(128)(4,1)S(1)}, s32[]{:S(2)}) async-start(s8[4325376]{0:T(1024)(128)(4,1)} %bitcast.58), calls=%async_computation.5 | async-start | bytes 8388608
  226.7 1.1 slice-start.1
  247.7 177.5 %reduce-scatter.7.cloned.1.call-start = ((), (), s32[]{:S(2)}) async-start(), calls=%async_computation.3 | async-start | bytes 12976128 | tf_op jit(solution)/shard_map/reduce_scatter | solution.py:74
  271.1 154.1 %copy-start = (f32[176,2,2048]{2,1,0:T(2,128)S(1)}, f32[176,2,2048]{2,1,0:T(2,128)}, u32[]{:S(2)}) copy-start(f32[176,2,2048]{2,1,0:T(2,128)} %param.11) | copy-start | bytes 8650756
Sparse Core Ops, SparseCore 0:
  247.8 86.6 reduce-scatter.8
  338.0 87.1 reduce-scatter.6
